TPU v7x, 128 devices: a whole 4x4x4 slice. The times are simulated.
128 devices in a mesh: obs: 8 (over z_hi, y), unk: 16 (over z_lo, x, core).
Axes of the slice: x: 4, y: 4, z: 4 (z_hi: 2, z_lo: 2; z = z_hi * 2 + z_lo), core: 2. Of those that a mesh axis runs over, the one named last changes fastest.
Arguments:
- design: float32 [8192, 24576], P('obs', 'unk'), may hold values from -0.0625 to 0.0625
- weights: float32 [8192], P('obs'), may hold values from 0.25 to 4
Outputs:
- factor: float32 [24576, 1024], P(('unk', 'obs'))
All inputs are finite; a program needn't handle non-finite values.
Results may differ from a plain program's by a relative error of at most 0.00011.
Values sent between devices are 32-bit elements; how exact they have to be, the bound alone decides.
No kernel may reach another device: no remote copies, remote signals or barrier semaphores. Data moves between devices by JAX's collectives and lax.ppermute only.
A program may use at most 128 MiB of HBM per device.

v0:
```python
import jax
import jax.numpy as jnp
from jax import lax
from jax.sharding import PartitionSpec as P

PANEL = 512
BLOCK = 128


def spread(block, axis, holder):
    block = jnp.where(lax.axis_index(axis) == holder, block, jnp.zeros_like(block))
    return lax.psum(block, axis)


def apply_lower(diag_factor, values):
    return lax.linalg.triangular_solve(
        diag_factor, values, left_side=False, lower=True, transpose_a=True
    )


def left_looking(top_block, owned_rows):
    width = top_block.shape[0]
    factor_top = jnp.zeros_like(top_block)
    factor_rows = jnp.zeros_like(owned_rows)
    for column_block in range(width // BLOCK):
        offset = column_block * BLOCK
        update_top = top_block[:, offset : offset + BLOCK]
        update_rows = owned_rows[:, offset : offset + BLOCK]
        if offset > 0:
            earlier = factor_top[offset : offset + BLOCK, :offset]
            update_top = update_top - jnp.dot(
                factor_top[:, :offset],
                earlier.T,
                precision=lax.Precision.HIGHEST,
                preferred_element_type=jnp.float32,
            )
            update_rows = update_rows - jnp.dot(
                factor_rows[:, :offset],
                earlier.T,
                precision=lax.Precision.HIGHEST,
                preferred_element_type=jnp.float32,
            )
        diag_factor = jnp.linalg.cholesky(update_top[offset : offset + BLOCK])
        below_top = apply_lower(diag_factor, update_top[offset + BLOCK :])
        new_column = jnp.concatenate(
            [jnp.zeros((offset, BLOCK), jnp.float32), diag_factor, below_top], axis=0
        )
        factor_top = factor_top.at[:, offset : offset + BLOCK].set(new_column)
        factor_rows = factor_rows.at[:, offset : offset + BLOCK].set(
            apply_lower(diag_factor, update_rows)
        )
    return factor_rows


def local(design, weights):
    panel_cols = spread(design[:, : 2 * PANEL], "unk", 0)
    weighted = panel_cols * weights[:, None]
    partial_value = lax.dot_general(
        design,
        weighted,
        (((0,), (0,)), ((), ())),
        precision=lax.Precision.HIGHEST,
        preferred_element_type=jnp.float32,
    )
    owned_rows = lax.psum_scatter(partial_value, "obs", scatter_dimension=0, tiled=True)
    gathered = lax.all_gather(owned_rows, "obs", axis=0, tiled=True)
    top_block = spread(gathered[: 2 * PANEL], "unk", 0)
    return left_looking(top_block, owned_rows)


def solution(mesh):
    return jax.shard_map(
        local,
        mesh=mesh,
        in_specs=(P("obs", "unk"), P("obs")),
        out_specs=P(("unk", "obs"), None),
        check_vma=False,
    )
```

profile of v0, /device:TPU:7, one launch (start us, length us, event | category | flops | bytes accessed | tf_op | source)
XLA Modules:
  0.0 775.2 jit_solution(10792649230344124611)
XLA Ops:
  6.5 4.7 slice.463
  11.3 5.3 copy.46
  16.6 2.8 broadcast_select_fusion.1
  19.5 132.4 %all-reduce.5.cloned.1.call-done = f32[1024,1024]{0,1:T(8,128)} async-done(((f32[1024,1024]{0,1:T(8,128)}), f32[1024,1024]{0,1:T(8,128)}) %all-reduce.5.cloned.1.call-update) | async-done | bytes 4194320 | tf_op jit(solution)/shard_map/psum | solution.py:12
  151.9 24.3 %convolution_bitcast_fusion = f32[1536,1024]{0,1:T(8,128)} fusion(f32[1024,1536]{1,0:T(8,128)} %param.35, f32[1024,1024]{0,1:T(8,128)} %all-reduce.5.cloned.1.call-done, f32[1024]{0:T(1024)S(1)} %copy-done.3), kind=kOutput, calls=%fused_computation | convolution fusion | flops 19328401408 | bytes 16781312 | tf_op jit(solution)/shard_map/dot_general | solution.py:58
  176.3 6.5 copy.44
  182.9 98.6 %reduce-scatter.4.cloned.1.call-done = f32[192,1024]{1,0:T(8,128)} async-done(((f32[1536,1024]{1,0:T(8,128)}), f32[192,1024]{1,0:T(8,128)}) %reduce-scatter.4.cloned.1.call-update) | async-done | bytes 786448 | tf_op jit(solution)/shard_map/reduce_scatter | solution.py:65
  281.5 90.1 %all-gather.2.cloned.1.call-done = f32[1536,1024]{1,0:T(8,128)} async-done(((f32[192,1024]{1,0:T(8,128)}), f32[1536,1024]{1,0:T(8,128)}) %all-gather.2.cloned.1.call-update) | async-done | bytes 6291472 | tf_op jit(solution)/shard_map/all_gather | solution.py:66
  371.6 4.7 slice.519
  376.3 5.3 copy.47
  381.7 2.8 broadcast_select_fusion
  385.9 0.7 compare_reduce_fusion.12
  388.5 1.1 compare_reduce_fusion.8
  390.4 122.7 %all-reduce.7.cloned.1.call-done = f32[1024,1024]{0,1:T(8,128)} async-done(((f32[1024,1024]{0,1:T(8,128)}), f32[1024,1024]{0,1:T(8,128)}) %all-reduce.7.cloned.1.call-update) | async-done | bytes 4194320 | tf_op jit(solution)/shard_map/psum | solution.py:12
  513.1 0.8 slice.520
  514.0 0.9 fusion.101
  514.9 11.7 %cholesky.134 = f32[128,128]{1,0:T(8,128)S(1)} custom-call(f32[128,128]{1,0:T(8,128)S(1)} %fusion.101), custom_call_target="Cholesky" | custom-call | tf_op jit(solution)/shard_map/jit(cholesky)/cholesky | solution.py:43
  527.9 9.8 %custom-call.40 = f32[1,128,128]{1,2,0:T(8,128)S(1)} custom-call(f32[1,128,128]{2,1,0:T(8,128)S(1)} %get-tuple-element.199), custom_call_target="InvertDiagBlocksLowerTriangular" | custom-call | tf_op jit(solution)/shard_map/triangular_solve/custom-call.0 | solution.py:16
  537.7 1.0 fusion.37
  538.8 2.1 fusion.48
  541.6 2.5 scatter.54
  545.2 11.9 %cholesky.145 = f32[128,128]{1,0:T(8,128)S(1)} custom-call(f32[128,128]{1,0:T(8,128)S(1)} %fusion.98), custom_call_target="Cholesky" | custom-call | tf_op jit(solution)/shard_map/jit(cholesky)/cholesky | solution.py:43
  558.4 9.8 %custom-call.41 = f32[1,128,128]{1,2,0:T(8,128)S(1)} custom-call(f32[1,128,128]{2,1,0:T(8,128)S(1)} %get-tuple-element.197), custom_call_target="InvertDiagBlocksLowerTriangular" | custom-call | tf_op jit(solution)/shard_map/triangular_solve/custom-call.0 | solution.py:16
  568.2 0.8 fusion.53
  569.1 1.5 fusion.46
  570.6 2.6 convolution_subtract_fusion
  573.4 11.7 %cholesky.156 = f32[128,128]{1,0:T(8,128)S(1)} custom-call(f32[128,128]{1,0:T(8,128)S(1)} %fusion.95), custom_call_target="Cholesky" | custom-call | tf_op jit(solution)/shard_map/jit(cholesky)/cholesky | solution.py:43
  586.4 9.8 %custom-call.42 = f32[1,128,128]{1,2,0:T(8,128)S(1)} custom-call(f32[1,128,128]{2,1,0:T(8,128)S(1)} %get-tuple-element.195), custom_call_target="InvertDiagBlocksLowerTriangular" | custom-call | tf_op jit(solution)/shard_map/triangular_solve/custom-call.0 | solution.py:16
  596.2 0.7 fusion.57
  596.9 1.0 fusion.36
  597.9 1.3 convolution_subtract_fusion.8
  599.2 1.2 fusion.34
  600.4 2.7 fusion.45
  603.1 3.4 fusion.15
  606.6 11.7 %cholesky.167 = f32[128,128]{1,0:T(8,128)S(1)} custom-call(f32[128,128]{1,0:T(8,128)S(1)} %fusion.92), custom_call_target="Cholesky" | custom-call | tf_op jit(solution)/shard_map/jit(cholesky)/cholesky | solution.py:43
  619.7 9.8 %custom-call.43 = f32[1,128,128]{1,2,0:T(8,128)S(1)} custom-call(f32[1,128,128]{2,1,0:T(8,128)S(1)} %get-tuple-element.193), custom_call_target="InvertDiagBlocksLowerTriangular" | custom-call | tf_op jit(solution)/shard_map/triangular_solve/custom-call.0 | solution.py:16
  630.1 1.5 convolution_subtract_fusion.5
  631.6 1.0 fusion.32
  632.6 2.7 fusion.44
  635.3 4.0 fusion.21
  639.5 12.1 %cholesky.178 = f32[128,128]{1,0:T(8,128)S(1)} custom-call(f32[128,128]{1,0:T(8,128)S(1)} %fusion.89), custom_call_target="Cholesky" | custom-call | tf_op jit(solution)/shard_map/jit(cholesky)/cholesky | solution.py:43
  652.9 9.8 %custom-call.44 = f32[1,128,128]{1,2,0:T(8,128)S(1)} custom-call(f32[1,128,128]{2,1,0:T(8,128)S(1)} %get-tuple-element.191), custom_call_target="InvertDiagBlocksLowerTriangular" | custom-call | tf_op jit(solution)/shard_map/triangular_solve/custom-call.0 | solution.py:16
  663.2 1.5 convolution_subtract_fusion.4
  664.7 1.0 fusion.30
  665.7 2.7 fusion.43
  668.3 4.7 fusion.18
  673.2 11.8 %cholesky.189 = f32[128,128]{1,0:T(8,128)S(1)} custom-call(f32[128,128]{1,0:T(8,128)S(1)} %fusion.86), custom_call_target="Cholesky" | custom-call | tf_op jit(solution)/shard_map/jit(cholesky)/cholesky | solution.py:43
  686.4 9.8 %custom-call.45 = f32[1,128,128]{1,2,0:T(8,128)S(1)} custom-call(f32[1,128,128]{2,1,0:T(8,128)S(1)} %get-tuple-element.189), custom_call_target="InvertDiagBlocksLowerTriangular" | custom-call | tf_op jit(solution)/shard_map/triangular_solve/custom-call.0 | solution.py:16
  696.6 1.7 convolution_subtract_fusion.3
  698.2 1.0 fusion.28
  699.2 2.7 fusion.42
  702.0 5.4 fusion.12
  707.5 11.7 %cholesky.200 = f32[128,128]{1,0:T(8,128)S(1)} custom-call(f32[128,128]{1,0:T(8,128)S(1)} %fusion.83), custom_call_target="Cholesky" | custom-call | tf_op jit(solution)/shard_map/jit(cholesky)/cholesky | solution.py:43
  720.6 10.0 %custom-call.46 = f32[1,128,128]{1,2,0:T(8,128)S(1)} custom-call(f32[1,128,128]{2,1,0:T(8,128)S(1)} %get-tuple-element.187), custom_call_target="InvertDiagBlocksLowerTriangular" | custom-call | tf_op jit(solution)/shard_map/triangular_solve/custom-call.0 | solution.py:16
  730.9 1.8 convolution_subtract_fusion.2
  732.7 0.9 fusion.26
  733.7 2.6 fusion.41
  736.3 6.0 fusion.1
  742.4 11.7 %cholesky.211 = f32[128,128]{1,0:T(8,128)S(1)} custom-call(f32[128,128]{1,0:T(8,128)S(1)} %fusion.80), custom_call_target="Cholesky" | custom-call | tf_op jit(solution)/shard_map/jit(cholesky)/cholesky | solution.py:43
  754.2 0.7 compare_reduce_fusion
  754.9 0.7 fusion.76
  755.6 9.8 %custom-call.47 = f32[1,128,128]{1,2,0:T(8,128)S(1)} custom-call(f32[1,128,128]{2,1,0:T(8,128)S(1)} %fusion.76), custom_call_target="InvertDiagBlocksLowerTriangular" | custom-call | tf_op jit(solution)/shard_map/triangular_solve/custom-call.0 | solution.py:16
  765.4 1.9 convolution_subtract_fusion.6
  767.4 1.0 fusion.24
  (94 shorter events, 17.9 us)
Async XLA Ops:
  6.5 145.4 %all-reduce.5.cloned.1.call-start = ((), (), s32[]{:S(2)}) async-start(), calls=%async_computation.1 | async-start | bytes 8388608 | tf_op jit(solution)/shard_map/psum | solution.py:12
  19.4 132.5 %copy-start.3 = (f32[1024]{0:T(1024)S(1)}, f32[1024]{0:T(1024)}, u32[]{:S(2)}) copy-start(f32[1024]{0:T(1024)} %param.36) | copy-start | bytes 12292
  19.4 262.0 %reduce-scatter.4.cloned.1.call-start = ((), (), s32[]{:S(2)}) async-start(), calls=%async_computation.4 | async-start | bytes 7077888 | tf_op jit(solution)/shard_map/reduce_scatter | solution.py:65
  182.8 188.8 %all-gather.2.cloned.1.call-start = ((), (), s32[]{:S(2)}) async-start(), calls=%async_computation.2 | async-start | bytes 7077888 | tf_op jit(solution)/shard_map/all_gather | solution.py:66
  281.5 231.6 %all-reduce.7.cloned.1.call-start = ((), (), s32[]{:S(2)}) async-start(), calls=%async_computation.3 | async-start | bytes 8388608 | tf_op jit(solution)/shard_map/psum | solution.py:12
  384.5 5.1 copy-start.2
  537.7 6.7 copy-start.1
  730.9 11.4 %slice-start = ((f32[1024,1024]{0,1:T(8,128)}), f32[1024,128]{0,1:T(8,128)S(1)}, s32[]{:S(2)}) async-start(f32[1024,1024]{0,1:T(8,128)} %all-reduce.7.cloned.1.call-done), calls=%async_computation.5 | async-start | bytes 1048576 | tf_op jit(solution)/shard_map/slice | solution.py:27
  733.6 33.7 %copy-start = (f32[192,1024]{1,0:T(8,128)}, f32[192,1024]{1,0:T(8,128)S(1)}, u32[]{:S(2)}) copy-start(f32[192,1024]{1,0:T(8,128)S(1)} %fusion.26) | copy-start | bytes 2359300
Sparse Core Ops, SparseCore 0:
  19.5 132.3 all-reduce.4
  182.9 98.4 reduce-scatter.3
  283.7 87.8 all-gather.1
  384.6 128.3 all-reduce.6
where the time goes:
time: 783 us; the launch traced here: 775 us
  waiting for transfers between devices  444 us (57%)
  other arithmetic  211 us (27%)
  matrix products  74.5 us (10%)
  local copies, waits for them, and re-layouts  31.6 us (4%)
  between operations  14.1 us (2%)
    psum x2, waiting for transfers between devices, spread(): return lax.psum(block, axis)  255 us
    another operation x24, other arithmetic, left_looking(): diag_factor = jnp.linalg.cholesky(update_top[offset:offset + BLOCK])  99.8 us
    reduce_scatter x1, waiting for transfers between devices, local(): lax.psum_scatter(partial_value, 'obs', scatter_dimension=0, tiled=True)  98.6 us
    all_gather x1, waiting for transfers between devices, local(): gathered = lax.all_gather(owned_rows, 'obs', axis=0, tiled=True)  90.1 us
    another operation x16, other arithmetic, apply_lower(): lax.linalg.triangular_solve(diag_factor, values, left_side=False, lower=T...  84 us
    dot_general x7, matrix products, left_looking(): jnp.dot(factor_top[:, :offset], earlier.T, precision=lax.Precision.HIGHES...  26.8 us
    dot_general x1, matrix products, local(): lax.dot_general(design, weighted, (((0,), (0,)), ((), ())), precision=lax...  24.3 us
    unnamed x18, local copies, waits for them, and re-layouts  17.9 us
  transfers between devices with their start and end apart: 4, of which 4 were waited for; matrix products, arithmetic and copies ran while one was open for 1% of the time, Pallas kernels for 0%

commit v1 on v0

--- a/solution.py
+++ b/solution.py
@@ -9,7 +9,7 @@
 
 def spread(block, axis, holder):
     block = jnp.where(lax.axis_index(axis) == holder, block, jnp.zeros_like(block))
-    return lax.psum(block, axis)
+    return jnp.sum(lax.all_gather(block, axis), axis=0)
 
 
 def apply_lower(diag_factor, values):

time: 783 us -> 1230 us (1.57)
  waiting for transfers between devices: 444 us -> 842 us
  other arithmetic: 211 us -> 264 us
    all_gather x0 -> x2, waiting for transfers between devices: none -> 652 us  [spread(): return jnp.sum(lax.all_gather(block, axis), axis=0)]
    psum x2 -> x0, waiting for transfers between devices: 255 us -> none  [spread(): return lax.psum(block, axis)]
    reduce_sum x0 -> x2, other arithmetic: none -> 46.3 us  [spread(): return jnp.sum(lax.all_gather(block, axis), axis=0)]
  transfers between devices with their start and end apart: 4 -> 4, of which waited for: 4 -> 4; matrix products, arithmetic and copies ran while one was open for 1% -> 0% of each run, Pallas kernels for 0% -> 0%
where the time goes in v1:
time: 1230 us; the launch traced here: 1220 us
  waiting for transfers between devices  842 us (68%)
  other arithmetic  264 us (21%)
  matrix products  75.6 us (6%)
  local copies, waits for them, and re-layouts  27.5 us (2%)
  between operations  14 us (1%)
    all_gather x2, waiting for transfers between devices, spread(): return jnp.sum(lax.all_gather(block, axis), axis=0)  652 us
    another operation x24, other arithmetic, left_looking(): diag_factor = jnp.linalg.cholesky(update_top[offset:offset + BLOCK])  99.6 us
    reduce_scatter x1, waiting for transfers between devices, local(): lax.psum_scatter(partial_value, 'obs', scatter_dimension=0, tiled=True)  99.1 us
    all_gather x1, waiting for transfers between devices, local(): gathered = lax.all_gather(owned_rows, 'obs', axis=0, tiled=True)  90.2 us
    another operation x16, other arithmetic, apply_lower(): lax.linalg.triangular_solve(diag_factor, values, left_side=False, lower=T...  84.4 us
    reduce_sum x2, other arithmetic, spread(): return jnp.sum(lax.all_gather(block, axis), axis=0)  46.3 us
    dot_general x7, matrix products, left_looking(): jnp.dot(factor_top[:, :offset], earlier.T, precision=lax.Precision.HIGHES...  26.5 us
  transfers between devices with their start and end apart: 4, of which 4 were waited for; matrix products, arithmetic and copies ran while one was open for 0% of the time, Pallas kernels for 0%

profile of v1, /device:TPU:7, one launch (start us, length us, event | category | flops | bytes accessed | tf_op | source)
XLA Modules:
  0.0 1223.2 jit_solution(13630293304010560138)
XLA Ops:
  6.5 5.0 slice_select_fusion.1
  11.6 330.8 %all-gather.8.cloned.1.call-done = f32[16384,1024]{1,0:T(8,128)} async-done(((f32[1024,1024]{1,0:T(8,128)}), f32[16384,1024]{1,0:T(8,128)}) %all-gather.8.cloned.1.call-update) | async-done | bytes 67108880 | tf_op jit(solution)/shard_map/all_gather | solution.py:12
  342.4 22.9 %reduce_sum.18 = f32[1024,1024]{1,0:T(8,128)} reduce(f32[16,1024,1024]{2,1,0:T(8,128)} %bitcast, f32[]{:T(128)} %constant.415.clone.1), dimensions={0}, to_apply=%region_1.2 | reduce | flops 15728640 | bytes 71303168 | tf_op jit(solution)/shard_map/reduce_sum | solution.py:12
  365.3 5.4 copy.77
  370.7 24.3 %convolution_bitcast_fusion = f32[1536,1024]{0,1:T(8,128)} fusion(f32[1024,1536]{1,0:T(8,128)} %param.35, f32[1024,1024]{0,1:T(8,128)} %copy.77, f32[1024]{0:T(1024)S(1)} %copy-done.11), kind=kOutput, calls=%fused_computation | convolution fusion | flops 19328401408 | bytes 16781312 | tf_op jit(solution)/shard_map/dot_general | solution.py:58
  395.0 6.5 copy.75
  401.6 99.1 %reduce-scatter.4.cloned.1.call-done = f32[192,1024]{1,0:T(8,128)} async-done(((f32[1536,1024]{1,0:T(8,128)}), f32[192,1024]{1,0:T(8,128)}) %reduce-scatter.4.cloned.1.call-update) | async-done | bytes 786448 | tf_op jit(solution)/shard_map/reduce_scatter | solution.py:65
  500.8 90.2 %all-gather.6.cloned.1.call-done = f32[1536,1024]{1,0:T(8,128)} async-done(((f32[192,1024]{1,0:T(8,128)}), f32[1536,1024]{1,0:T(8,128)}) %all-gather.6.cloned.1.call-update) | async-done | bytes 6291472 | tf_op jit(solution)/shard_map/all_gather | solution.py:66
  590.9 5.0 slice_select_fusion
  601.3 321.6 %all-gather.10.cloned.1.call-done = f32[16384,1024]{1,0:T(8,128)} async-done(((f32[1024,1024]{1,0:T(8,128)}), f32[16384,1024]{1,0:T(8,128)}) %all-gather.10.cloned.1.call-update) | async-done | bytes 67108880 | tf_op jit(solution)/shard_map/all_gather | solution.py:12
  922.8 23.4 %reduce_sum.19 = f32[1024,1024]{1,0:T(8,128)} reduce(f32[16,1024,1024]{2,1,0:T(8,128)} %bitcast.2, f32[]{:T(128)} %constant.415.clone.1), dimensions={0}, to_apply=%region_3.4 | reduce | flops 15728640 | bytes 71303168 | tf_op jit(solution)/shard_map/reduce_sum | solution.py:12
  947.1 3.0 fusion.107
  950.2 1.5 fusion.106
  951.7 11.7 cholesky.134
  964.7 9.8 custom-call.40
  974.5 1.6 fusion.48
  976.1 1.0 copy.80
  977.8 2.5 scatter.54
  981.8 0.9 fusion.98
  982.7 11.7 cholesky.145
  995.7 9.9 custom-call.41
  1005.7 1.8 fusion.53
  1007.5 1.0 copy.81
  1008.5 1.5 fusion.46
  1010.0 2.6 convolution_subtract_fusion
  1012.8 11.7 cholesky.156
  1025.2 1.2 select_bitcast_fusion.4
  1026.5 9.8 custom-call.42
  1038.6 2.1 copy.82
  1040.7 1.2 convolution_subtract_fusion.6
  1041.8 1.8 fusion.36
  1043.6 1.2 convolution_subtract_fusion.8
  1044.8 1.0 fusion.34
  1045.8 3.0 fusion.45
  1048.8 3.4 fusion.15
  1053.9 11.7 cholesky.167
  1066.8 9.8 custom-call.43
  1076.6 1.5 fusion.62
  1078.2 1.0 copy.83
  1079.2 1.4 convolution_subtract_fusion.7
  1080.6 0.9 fusion.32
  1081.4 2.7 fusion.44
  1084.1 4.0 fusion.21
  1088.3 12.1 cholesky.178
  1101.7 9.8 custom-call.44
  1112.3 1.4 convolution_subtract_fusion.5
  1113.7 0.9 fusion.30
  1114.6 2.8 fusion.43
  1117.4 4.6 fusion.18
  1122.1 11.9 cholesky.189
  1135.3 9.8 custom-call.45
  1145.7 1.6 convolution_subtract_fusion.4
  1148.1 2.6 fusion.42
  1150.7 5.3 fusion.12
  1156.2 11.7 cholesky.200
  1169.2 10.0 custom-call.46
  1179.5 1.6 convolution_subtract_fusion.3
  1181.2 0.9 fusion.26
  1182.0 2.7 fusion.41
  1184.7 6.0 fusion.1
  1191.0 11.7 cholesky.211
  1204.0 9.8 custom-call.47
  1213.8 1.8 convolution_subtract_fusion.2
  1215.6 0.9 fusion.24
  (107 shorter events, 25.5 us)
Async XLA Ops:
  6.5 335.9 %all-gather.8.cloned.1.call-start = ((), (), s32[]{:S(2)}) async-start(), calls=%async_computation.2 | async-start | bytes 71303168 | tf_op jit(solution)/shard_map/all_gather | solution.py:12
  11.5 489.1 %reduce-scatter.4.cloned.1.call-start = ((), (), s32[]{:S(2)}) async-start(), calls=%async_computation.4 | async-start | bytes 7077888 | tf_op jit(solution)/shard_map/reduce_scatter | solution.py:65
  365.3 5.4 copy-start.11
  401.6 189.3 %all-gather.6.cloned.1.call-start = ((), (), s32[]{:S(2)}) async-start(), calls=%async_computation.1 | async-start | bytes 7077888 | tf_op jit(solution)/shard_map/all_gather | solution.py:66
  500.7 422.1 %all-gather.10.cloned.1.call-start = ((), (), s32[]{:S(2)}) async-start(), calls=%async_computation.3 | async-start | bytes 71303168 | tf_op jit(solution)/shard_map/all_gather | solution.py:12
  974.5 2.6 copy-start.9
  977.1 3.2 copy-start.4
  980.3 56.7 %copy-start.1 = (f32[192,1024]{1,0:T(8,128)S(1)}, f32[192,1024]{1,0:T(8,128)}, u32[]{:S(2)}) copy-start(f32[192,1024]{1,0:T(8,128)} %reduce-scatter.4.cloned.1.call-done) | copy-start | bytes 2359300
  980.3 56.7 %copy-start.10 = (f32[1,128,128]{1,2,0:T(8,128)S(1)}, f32[1,128,128]{1,2,0:T(8,128)}, u32[]{:S(2)}) copy-start(f32[1,128,128]{1,2,0:T(8,128)} %copy-done.9) | copy-start | bytes 196612
  980.9 0.8 copy-start.3
  1005.6 7.0 copy-start.8
  1037.9 0.6 copy-start.6
  1041.8 36.4 %copy-start.2 = (f32[1024,128]{1,0:T(8,128)S(1)}, f32[1024,128]{1,0:T(8,128)}, u32[]{:S(2)}) copy-start(f32[1024,128]{1,0:T(8,128)} %get-tuple-element.205) | copy-start | bytes 1572868
  1052.1 0.8 copy-start.5
  1156.0 34.7 %copy-start.7 = (f32[128,128]{1,0:T(8,128)S(1)}, f32[128,128]{1,0:T(8,128)}, u32[]{:S(2)}) copy-start(f32[128,128]{1,0:T(8,128)} %get-tuple-element.201) | copy-start | bytes 196612
  1182.0 33.6 %copy-start = (f32[192,1024]{1,0:T(8,128)}, f32[192,1024]{1,0:T(8,128)S(1)}, u32[]{:S(2)}) copy-start(f32[192,1024]{1,0:T(8,128)S(1)} %fusion.26) | copy-start | bytes 2359300
Sparse Core Ops, SparseCore 0:
  11.7 330.6 all-gather.7
  401.7 98.9 reduce-scatter.3
  503.0 87.8 all-gather.5
  596.0 326.7 all-gather.9
